TPU v7x, 32 devices: a whole 2x2x4 slice. The times are simulated.
32 devices in a mesh: rep: 2 (over x), idx: 16 (over z, y, core).
Axes of the slice: x: 2, y: 2, z: 4, core: 2. Of those that a mesh axis runs over, the one named last changes fastest.
Arguments:
- images: bfloat16 [16448, 1408], P(('rep', 'idx')), parts along dimension 0, may hold values from -6 to 6
- norm_gain: float32 [1408], replicated, may hold values from 0.25 to 1.75
- qkv_values: bfloat16 [1408, 4224], P(None, 'idx'), may hold values from -0.5 to 0.5
- qkv_exponents: int32 [11, 4224], replicated, may hold values from -2 to 2
- proj_values: bfloat16 [1408, 1408], P(None, 'idx'), may hold values from -0.078125 to 0.078125
- proj_exponents: int32 [11, 1408], replicated, may hold values from -2 to 2
- captions: bfloat16 [32768, 1408], P(('rep', 'idx')), parts along dimension 0, may hold values from -0.15625 to 0.15625
- owners: int32 [16448, 1], P(('rep', 'idx')), parts along dimension 0, may hold values from 0 to 15; in each aligned block of 514 rows (0 to 513, 514 to 1027, ...) at most 34 rows name the same one
- candidates: int32 [16448, 4], P(('rep', 'idx')), parts along dimension 0, may hold values from 0 to 7, all different within a row
Outputs:
- embedding: bfloat16 [16448, 1408], P(('rep', 'idx')), parts along dimension 0
- scores: bfloat16 [16448, 4, 128], P(('rep', 'idx')), parts along dimension 0
There are 2 independent parts, one for each index of `rep`. A program takes and returns all parts, laid end to end along the dimension named above; an argument that names none is the same for every part. Nothing has to cross between parts.
Inputs may be any that keep to these rules, and one draw needn't show every extreme that they name: `owners`: among the tokens of one device no owner is named more than 34 times, a bound that some block reaches. `candidates`: each token names 4 different caption blocks.
All inputs are finite; a program needn't handle non-finite values.
Results may differ from a plain program's by a relative error of at most 0.004.
The roundings to bfloat16 on the way count: a program that leaves them out, or rounds other values in their place, can miss the bound.
Values may be sent and summed in bfloat16 or wider, within the bound.
A program may use at most 192 MiB of HBM per device.

v0:
```python
import jax
import jax.numpy as jnp
from jax import lax
from jax.sharding import PartitionSpec as P

HEADS = 16
PATCHES = 257
CBLK = 8
CAPT = 128


def dequant(stored, exponents):
    row_count, col_count = stored.shape
    block_count = exponents.shape[0]
    scaled = stored.astype(jnp.float32).reshape(block_count, row_count // block_count, col_count)
    scaled = scaled * jnp.exp2(exponents.astype(jnp.float32))[:, None, :]
    return scaled.reshape(row_count, col_count).astype(jnp.bfloat16)


def layer_norm(token_rows, norm_gain):
    values = token_rows.astype(jnp.float32)
    centered = values - jnp.mean(values, axis=-1, keepdims=True)
    inv_scale = lax.rsqrt(jnp.mean(centered * centered, axis=-1, keepdims=True) + 1e-06)
    return (centered * inv_scale * norm_gain).astype(jnp.bfloat16)


def attend(qkv_rows, model_width):
    head_dim = model_width // HEADS
    grouped = qkv_rows.reshape(-1, PATCHES, 3, HEADS, head_dim)
    logits = jnp.einsum(
        "gqhd,gkhd->ghqk", grouped[:, :, 0], grouped[:, :, 1], preferred_element_type=jnp.float32
    )
    logits = logits * head_dim ** (-0.5)
    logits = logits - jnp.max(logits, axis=-1, keepdims=True)
    weights = jnp.exp(logits)
    attn_probs = (weights / jnp.sum(weights, axis=-1, keepdims=True)).astype(jnp.bfloat16)
    mixed_heads = jnp.einsum(
        "ghqk,gkhd->gqhd", attn_probs, grouped[:, :, 2], preferred_element_type=jnp.float32
    )
    return mixed_heads.astype(jnp.bfloat16).reshape(-1, model_width)


def project_with(left_rows, exponents, col_piece):
    return jnp.dot(left_rows, dequant(col_piece, exponents), preferred_element_type=jnp.float32)


def score_with(captions):

    def score_slots(slot_parts):
        slot_rows, slot_picks = slot_parts
        peer_count, item_count = (slot_rows.shape[0], slot_rows.shape[1])
        flat_rows = slot_rows.reshape(peer_count * item_count, slot_rows.shape[2])
        all_scores = lax.dot_general(
            flat_rows, captions, (((1,), (1,)), ((), ())), preferred_element_type=jnp.float32
        )
        all_scores = all_scores.reshape(peer_count * item_count, CBLK, CAPT)
        block_index = jnp.clip(
            slot_picks.reshape(peer_count * item_count, -1).astype(jnp.int32), 0, CBLK - 1
        )
        chosen = jnp.take_along_axis(all_scores, block_index[:, :, None], axis=1)
        return chosen.astype(jnp.bfloat16).reshape(peer_count, item_count, -1, CAPT)

    return score_slots


def local(
    images,
    norm_gain,
    qkv_values,
    qkv_exponents,
    proj_values,
    proj_exponents,
    captions,
    owners,
    candidates,
):
    model_width = images.shape[1]
    normed = layer_norm(images, norm_gain)
    qkv_rows = project_with(
        normed, qkv_exponents, lax.all_gather(qkv_values, "idx", axis=1, tiled=True)
    ).astype(jnp.bfloat16)
    mixed_heads = attend(qkv_rows, model_width)
    branch = project_with(
        mixed_heads, proj_exponents, lax.all_gather(proj_values, "idx", axis=1, tiled=True)
    )
    hidden = images.astype(jnp.float32) + branch
    inv_scale = lax.rsqrt(jnp.mean(hidden * hidden, axis=-1, keepdims=True) + 1e-06)
    embedding = (hidden * inv_scale).astype(jnp.bfloat16)
    token_count = embedding.shape[0]
    peer_count = lax.axis_size("idx")
    capacity = (token_count + peer_count - 1) // peer_count + 1
    owner_ids = owners[:, 0]
    onehot = (owner_ids[:, None] == jnp.arange(peer_count, dtype=jnp.int32)[None, :]).astype(
        jnp.int32
    )
    slot_rank = jnp.sum((jnp.cumsum(onehot, axis=0) - onehot) * onehot, axis=1)
    slot_index = owner_ids * capacity + slot_rank
    send_rows = (
        jnp.zeros((peer_count * capacity, model_width), jnp.bfloat16).at[slot_index].set(embedding)
    )
    send_rows = send_rows.reshape(peer_count, capacity, model_width)
    pick_count = candidates.shape[1]
    send_picks = (
        jnp.full((peer_count * capacity, pick_count), -1.0, jnp.bfloat16)
        .at[slot_index]
        .set(candidates.astype(jnp.bfloat16))
    )
    send_picks = send_picks.reshape(peer_count, capacity, pick_count)
    score_slots = score_with(captions)
    arrived = (
        lax.all_to_all(send_rows, "idx", split_axis=0, concat_axis=0, tiled=True),
        lax.all_to_all(send_picks, "idx", split_axis=0, concat_axis=0, tiled=True),
    )
    returned = lax.all_to_all(score_slots(arrived), "idx", split_axis=0, concat_axis=0, tiled=True)
    scores = returned.reshape(peer_count * capacity, pick_count, CAPT)[slot_index]
    return (embedding, scores)


def solution(mesh):
    placed = (
        P(("rep", "idx"), None),
        P(),
        P(None, "idx"),
        P(),
        P(None, "idx"),
        P(),
        P(("rep", "idx"), None),
        P(("rep", "idx"), None),
        P(("rep", "idx"), None),
    )
    return jax.shard_map(
        local,
        mesh=mesh,
        in_specs=placed,
        out_specs=(P(("rep", "idx"), None), P(("rep", "idx"), None, None)),
        check_vma=False,
    )
```

profile of v0, /device:TPU:0, one launch (start us, length us, event | category | flops | bytes accessed | tf_op | source)
XLA Modules:
  0.0 386.6 jit_solution(72550061638257239)
XLA Ops:
  12.8 4.2 %scatter_custom_fusion = bf16[544,4]{1,0:T(8,128)(2,1)S(1)} fusion(s32[514]{0:T(1024)S(1)} %fusion.30, bf16[514,4]{1,0:T(8,128)(2,1)S(1)} %copy.41, bf16[]{:T(256)} %constant.14.clone.1), kind=kCustom, calls=%fused_computation.40 | custom fusion | bytes 4354 | tf_op jit(solution)/shard_map/scatter | solution.py:106
  17.9 7.4 %all-to-all-start = ((bf16[16,34,4]{1,2,0:T(4,128)(2,1)}), bf16[16,34,4]{1,2,0:T(4,128)(2,1)S(1)}, u32[]{:S(2)}, u32[]{:S(2)}) async-start(bf16[16,34,4]{1,2,0:T(4,128)(2,1)} %copy.43), calls=%async_computation | async-start | bytes 32768 | tf_op jit(solution)/shard_map/all_to_all | solution.py:112
  25.4 1.7 convert_reduce_fusion
  27.0 1.9 fusion.10
  29.1 33.5 %all-gather.5.cloned.1.call-done = bf16[1408,1408]{0,1:T(8,128)(2,1)} async-done(((bf16[1408,88]{0,1:T(8,128)(2,1)}), bf16[1408,1408]{0,1:T(8,128)(2,1)}) %all-gather.5.cloned.1.call-update) | async-done | bytes 3964944 | tf_op jit(solution)/shard_map/all_gather | solution.py:84
  62.6 6.2 %copy.38 = bf16[1408,1408]{1,0:T(8,128)(2,1)} copy(bf16[1408,1408]{0,1:T(8,128)(2,1)} %all-gather.5.cloned.1.call-done) | data formatting | bytes 7929856 | tf_op jit(solution)/shard_map/all_gather | solution.py:84
  68.8 5.0 %fusion.5 = bf16[1408,1408]{1,0:T(8,128)(2,1)} fusion(bf16[1408,1408]{1,0:T(8,128)(2,1)} %copy.38, f32[11,1408]{1,0:T(8,128)S(1)} %multiply_exponential_fusion.1), kind=kLoop, calls=%fused_computation.12 | loop fusion | flops 5947392 | bytes 7991808 | tf_op jit(solution)/shard_map/convert_element_type | solution.py:17
  73.8 85.8 %all-gather.3.cloned.1.call-done = bf16[1408,4224]{0,1:T(8,128)(2,1)} async-done(((bf16[1408,264]{0,1:T(8,128)(2,1)}), bf16[1408,4224]{0,1:T(8,128)(2,1)}) %all-gather.3.cloned.1.call-update) | async-done | bytes 11894800 | tf_op jit(solution)/shard_map/all_gather | solution.py:80
  159.6 16.0 %copy.32 = bf16[1408,4224]{1,0:T(8,128)(2,1)} copy(bf16[1408,4224]{0,1:T(8,128)(2,1)} %all-gather.3.cloned.1.call-done) | data formatting | bytes 23789568 | tf_op jit(solution)/shard_map/all_gather | solution.py:80
  175.6 6.8 %fusion.1 = bf16[1408,4224]{1,0:T(8,128)(2,1)S(1)} fusion(bf16[1408,4224]{1,0:T(8,128)(2,1)} %copy.32, f32[11,4224]{1,0:T(8,128)S(1)} %multiply_exponential_fusion), kind=kLoop, calls=%fused_computation.6 | loop fusion | flops 17842176 | bytes 23975424 | tf_op jit(solution)/shard_map/convert_element_type | solution.py:17
  182.4 9.2 %convolution_convert_fusion = bf16[514,4224]{1,0:T(8,128)(2,1)} fusion(bf16[1408,4224]{1,0:T(8,128)(2,1)S(1)} %fusion.1, bf16[514,1408]{1,0:T(8,128)(2,1)S(1)} %copy-done.1, f32[1408]{0:T(1024)S(1)} %copy-done.4, f32[514]{0:T(1024)S(1)} %add_rsqrt_fusion.1, f32[514]{0:T(1024)S(1)} %broadcast_multiply_fusion), kind=kOutput, calls=%fused_computation.13 | convolution fusion | flops 6119708672 | bytes 17694224 | tf_op jit(solution)/shard_map/dot_general | solution.py:44
  191.6 14.7 %reshape.106 = bf16[2,257,3,16,88]{4,3,2,1,0:T(8,128)(2,1)} reshape(bf16[514,4224]{1,0:T(8,128)(2,1)} %convolution_convert_fusion) | data formatting | bytes 8684544 | tf_op jit(solution)/shard_map/reshape | solution.py:29
  206.2 5.3 %fusion.32 = (bf16[2,257,1,16,88]{4,3,2,1,0:T(8,128)(2,1)}, bf16[2,257,1,16,88]{4,3,2,1,0:T(8,128)(2,1)S(1)}, bf16[2,257,1,16,88]{4,3,2,1,0:T(8,128)(2,1)S(1)}) fusion(bf16[2,257,3,16,88]{4,3,2,1,0:T(8,128)(2,1)} %reshape.106), kind=kLoop, calls=%fused_computation.65 | loop fusion | bytes 8684544 | tf_op jit(solution)/shard_map/slice | solution.py:38
  211.5 7.2 %fusion.13 = f32[2,16,257,257]{2,3,1,0:T(8,128)} fusion(bf16[2,257,1,16,88]{4,3,2,1,0:T(8,128)(2,1)S(1)} %get-tuple-element.3, bf16[2,257,1,16,88]{4,3,2,1,0:T(8,128)(2,1)S(1)} %get-tuple-element.4), kind=kOutput, calls=%fused_computation.27 | convolution fusion | flops 371987968 | bytes 11349120 | tf_op jit(solution)/shard_map/gqhd,gkhd->ghqk/dot_general | solution.py:30
  218.7 16.6 %fusion.33 = (f32[2,16,257]{2,1,0:T(8,128)S(1)}, f32[2,16,257,257]{2,3,1,0:T(8,128)}) fusion(f32[2,16,257,257]{2,3,1,0:T(8,128)} %fusion.13), kind=kOutput, calls=%fused_computation.66 | output fusion | flops 8454528 | bytes 16941440 | tf_op jit(solution)/shard_map/sub | solution.py:34
  235.3 4.4 %copy.49 = bf16[2,257,1,16,88]{1,4,3,0,2:T(8,128)(2,1)} copy(bf16[2,257,1,16,88]{4,3,2,1,0:T(8,128)(2,1)} %get-tuple-element.2) | data formatting | bytes 2894848
  239.8 8.5 %convert_bitcast_fusion = bf16[2,257,16,88]{1,3,2,0:T(8,128)(2,1)} fusion(f32[2,16,257,257]{2,3,1,0:T(8,128)} %get-tuple-element.6, f32[2,16,257]{2,1,0:T(8,128)S(1)} %get-tuple-element.5, bf16[2,257,1,16,88]{1,4,3,0,2:T(8,128)(2,1)} %copy.49), kind=kOutput, calls=%fused_computation.30 | convolution fusion | flops 376938816 | bytes 11382016 | tf_op jit(solution)/shard_map/ghqk,gkhd->gqhd/dot_general | solution.py:37
  248.3 4.5 %copy.37 = bf16[2,257,16,88]{3,2,1,0:T(8,128)(2,1)} copy(bf16[2,257,16,88]{1,3,2,0:T(8,128)(2,1)} %convert_bitcast_fusion) | data formatting | bytes 2894848 | tf_op jit(solution)/shard_map/convert_element_type | solution.py:40
  252.8 4.6 %reshape.107 = bf16[514,1408]{1,0:T(8,128)(2,1)} reshape(bf16[2,257,16,88]{3,2,1,0:T(8,128)(2,1)} %copy.37) | data formatting | bytes 2894848 | tf_op jit(solution)/shard_map/reshape | solution.py:40
  257.5 7.3 %multiply_reduce_fusion.1 = (f32[514]{0:T(1024)S(1)}, f32[514,1408]{1,0:T(8,128)}) fusion(bf16[514,1408]{1,0:T(8,128)(2,1)} %reshape.107, bf16[1408,1408]{1,0:T(8,128)(2,1)} %fusion.5, bf16[514,1408]{1,0:T(8,128)(2,1)} %param.9), kind=kOutput, calls=%fused_computation.25 | convolution fusion | flops 2040867328 | bytes 9756680 | tf_op jit(solution)/shard_map/dot_general | solution.py:44
  264.7 12.3 %scatter_custom_fusion.1 = bf16[544,1408]{1,0:T(8,128)(2,1)} fusion(s32[514]{0:T(1024)S(1)} %fusion.30, bf16[]{:T(256)} %constant.45.clone.1, f32[514,1408]{1,0:T(8,128)} %get-tuple-element.8, f32[514]{0:T(1024)S(1)} %add_rsqrt_fusion), kind=kCustom, calls=%fused_computation.35 | custom fusion | flops 1447424 | bytes 4430850 | tf_op jit(solution)/shard_map/scatter | solution.py:99
  277.0 2.6 reshape.111
  279.6 4.4 %all-to-all-start.1 = ((bf16[16,34,1408]{2,1,0:T(8,128)(2,1)}), bf16[16,34,1408]{2,1,0:T(8,128)(2,1)}, u32[]{:S(2)}, u32[]{:S(2)}) async-start(bf16[16,34,1408]{2,1,0:T(8,128)(2,1)} %reshape.111), calls=%async_computation.1 | async-start | bytes 3604480 | tf_op jit(solution)/shard_map/all_to_all | solution.py:111
  284.9 35.0 %all-to-all-done.1 = bf16[16,34,1408]{2,1,0:T(8,128)(2,1)} async-done(((bf16[16,34,1408]{2,1,0:T(8,128)(2,1)}), bf16[16,34,1408]{2,1,0:T(8,128)(2,1)}, u32[]{:S(2)}, u32[]{:S(2)}) %all-to-all-start.1) | async-done | bytes 1531936 | tf_op jit(solution)/shard_map/all_to_all | solution.py:111
  319.9 2.6 reshape.146
  322.5 3.3 fusion.34
  327.2 22.9 %gather_fusion.1 = bf16[2176,128]{1,0:T(8,128)(2,1)S(1)} fusion(bf16[544,8,128]{2,1,0:T(8,128)(2,1)} %copy.47, s32[2176]{0:T(1024)S(1)} %reshape.123), kind=kCustom, calls=%fused_computation.1 | custom fusion | bytes 1131520 | tf_op jit(solution)/shard_map/jit(take_along_axis)/gather | solution.py:60
  350.2 1.5 select_convert_fusion
  351.6 10.2 %all-to-all-start.2 = ((bf16[16,34,4,128]{3,2,1,0:T(4,128)(2,1)}), bf16[16,34,4,128]{3,2,1,0:T(4,128)(2,1)S(1)}, u32[]{:S(2)}, u32[]{:S(2)}) async-start(bf16[16,34,4,128]{3,2,1,0:T(4,128)(2,1)} %select_convert_fusion), calls=%async_computation.2 | async-start | bytes 1114112 | tf_op jit(solution)/shard_map/all_to_all | solution.py:114
  361.9 3.2 multiply_convert_fusion
  365.0 11.6 %all-to-all-done.2 = bf16[16,34,4,128]{3,2,1,0:T(4,128)(2,1)S(1)} async-done(((bf16[16,34,4,128]{3,2,1,0:T(4,128)(2,1)}), bf16[16,34,4,128]{3,2,1,0:T(4,128)(2,1)S(1)}, u32[]{:S(2)}, u32[]{:S(2)}) %all-to-all-start.2) | async-done | bytes 557088 | tf_op jit(solution)/shard_map/all_to_all | solution.py:114
  376.7 3.1 gather_fusion
  (44 shorter events, 8.7 us)
Async XLA Ops:
  7.2 315.3 %copy-start = (bf16[1024,1408]{1,0:T(8,128)(2,1)S(1)}, bf16[1024,1408]{1,0:T(8,128)(2,1)}, u32[]{:S(2)}) copy-start(bf16[1024,1408]{1,0:T(8,128)(2,1)} %param.15) | copy-start | bytes 8650756
  7.2 21.8 %copy-start.2 = (s32[11,4224]{1,0:T(8,128)S(1)}, s32[11,4224]{1,0:T(8,128)}, u32[]{:S(2)}) copy-start(s32[11,4224]{1,0:T(8,128)} %param.12) | copy-start | bytes 557572
  7.2 55.4 %all-gather.5.cloned.1.call-start = ((), (), s32[]{:S(2)}) async-start(), calls=%async_computation.4 | async-start | bytes 4212736 | tf_op jit(solution)/shard_map/all_gather | solution.py:84
  7.9 151.7 %all-gather.3.cloned.1.call-start = ((), (), s32[]{:S(2)}) async-start(), calls=%async_computation.3 | async-start | bytes 12638208 | tf_op jit(solution)/shard_map/all_gather | solution.py:80
  17.1 11.9 %copy-start.3 = (s32[11,1408]{1,0:T(8,128)S(1)}, s32[11,1408]{1,0:T(8,128)}, u32[]{:S(2)}) copy-start(s32[11,1408]{1,0:T(8,128)} %param.14) | copy-start | bytes 185860
  17.9 261.7 %all-to-all-start = ((bf16[16,34,4]{1,2,0:T(4,128)(2,1)}), bf16[16,34,4]{1,2,0:T(4,128)(2,1)S(1)}, u32[]{:S(2)}, u32[]{:S(2)}) async-start(bf16[16,34,4]{1,2,0:T(4,128)(2,1)} %copy.43), calls=%async_computation | async-start | bytes 32768 | tf_op jit(solution)/shard_map/all_to_all | solution.py:112
  175.5 6.8 %copy-start.1 = (bf16[514,1408]{1,0:T(8,128)(2,1)S(1)}, bf16[514,1408]{1,0:T(8,128)(2,1)}, u32[]{:S(2)}) copy-start(bf16[514,1408]{1,0:T(8,128)(2,1)} %param.9) | copy-start | bytes 4342276
  175.6 6.8 %copy-start.4 = (f32[1408]{0:T(1024)S(1)}, f32[1408]{0:T(1024)}, u32[]{:S(2)}) copy-start(f32[1408]{0:T(1024)} %param.10) | copy-start | bytes 16900
  279.6 40.3 %all-to-all-start.1 = ((bf16[16,34,1408]{2,1,0:T(8,128)(2,1)}), bf16[16,34,1408]{2,1,0:T(8,128)(2,1)}, u32[]{:S(2)}, u32[]{:S(2)}) async-start(bf16[16,34,1408]{2,1,0:T(8,128)(2,1)} %reshape.111), calls=%async_computation.1 | async-start | bytes 3604480 | tf_op jit(solution)/shard_map/all_to_all | solution.py:111
  351.6 25.0 %all-to-all-start.2 = ((bf16[16,34,4,128]{3,2,1,0:T(4,128)(2,1)}), bf16[16,34,4,128]{3,2,1,0:T(4,128)(2,1)S(1)}, u32[]{:S(2)}, u32[]{:S(2)}) async-start(bf16[16,34,4,128]{3,2,1,0:T(4,128)(2,1)} %select_convert_fusion), calls=%async_computation.2 | async-start | bytes 1114112 | tf_op jit(solution)/shard_map/all_to_all | solution.py:114
Sparse Core Ops, SparseCore 0:
  10.2 52.3 all-gather.4
  64.7 94.8 all-gather.2
where the time goes:
time: 388 us; the launch traced here: 387 us
  waiting for transfers between devices  167 us (43%)
  local copies, waits for them, and re-layouts  94.7 us (24%)
  other arithmetic  52.8 us (14%)
  matrix products  35.4 us (9%)
  starting transfers between devices  22.1 us (6%)
  between operations  14.3 us (4%)
    all_gather x1, waiting for transfers between devices, local(): lax.all_gather(qkv_values, 'idx', axis=1, tiled=True)  85.8 us
    all_to_all x1, waiting for transfers between devices, local(): lax.all_to_all(send_rows, 'idx', split_axis=0, concat_axis=0, tiled=True)  35 us
    all_gather x1, waiting for transfers between devices, local(): lax.all_gather(proj_values, 'idx', axis=1, tiled=True)  33.5 us
    gather x3, local copies, waits for them, and re-layouts, score_slots(): chosen = jnp.take_along_axis(all_scores, block_index[:, :, None], axis=1)  23.3 us
    sub x1, other arithmetic, attend(): logits = logits - jnp.max(logits, axis=-1, keepdims=True)  16.6 us
    dot_general x2, matrix products, project_with(): jnp.dot(left_rows, dequant(col_piece, exponents), preferred_element_type=...  16.4 us
    all_gather x1, local copies, waits for them, and re-layouts, local(): lax.all_gather(qkv_values, 'idx', axis=1, tiled=True)  16 us
    reshape x1, local copies, waits for them, and re-layouts, attend(): grouped = qkv_rows.reshape(-1, PATCHES, 3, HEADS, head_dim)  14.7 us
  transfers between devices with their start and end apart: 5, of which 4 were waited for; matrix products, arithmetic and copies ran while one was open for 38% of the time, Pallas kernels for 0%

commit v1 on v0

--- a/solution.py
+++ b/solution.py
@@ -7,6 +7,37 @@
 PATCHES = 257
 CBLK = 8
 CAPT = 128
+
+
+def vector_detail(my_tile, where_dim, mine_x):
+    outer = my_tile.shape
+    inter = my_tile.reshape(
+        *outer[:where_dim], mine_x, outer[where_dim] // mine_x, *outer[where_dim + 1 :]
+    )
+    return jnp.moveaxis(inter, where_dim, 0)
+
+
+def launch_orders(inp, join_dim):
+    low = list(inp.shape[1:])
+    low[join_dim] *= inp.shape[0]
+    return jnp.moveaxis(inp, 0, join_dim).reshape(low)
+
+
+def extend_the_tasks(shard_in, dev_axis, local_x, q_in):
+    block_last = lax.axis_index(dev_axis)
+    found_now = lax.axis_size(dev_axis)
+    row_out, response = (found_now, block_last)
+    arr_now = vector_detail(shard_in, local_x, row_out)
+    copies = [arr_now[response]]
+    for m in range(1, row_out):
+        y1 = arr_now[(response + m) % row_out]
+        current_value = lax.ppermute(
+            y1, axis_name=dev_axis, perm=[(w, (w + m) % row_out) for w in range(row_out)]
+        )
+        copies.append(current_value)
+    moved = jnp.stack(copies)
+    arr_now = moved[(response - jnp.arange(row_out)) % row_out]
+    return launch_orders(arr_now, q_in)
 
 
 def dequant(stored, exponents):
@@ -111,7 +142,7 @@
         lax.all_to_all(send_rows, "idx", split_axis=0, concat_axis=0, tiled=True),
         lax.all_to_all(send_picks, "idx", split_axis=0, concat_axis=0, tiled=True),
     )
-    returned = lax.all_to_all(score_slots(arrived), "idx", split_axis=0, concat_axis=0, tiled=True)
+    returned = extend_the_tasks(score_slots(arrived), "idx", 0, 0)
     scores = returned.reshape(peer_count * capacity, pick_count, CAPT)[slot_index]
     return (embedding, scores)
 

time: 388 us -> 407 us (1.049); the launches traced: 387 us -> 399 us
  starting transfers between devices: 22.1 us -> 40.8 us
  waiting for transfers between devices: 167 us -> 157 us
  local copies, waits for them, and re-layouts: 94.7 us -> 98.8 us
    ppermute x0 -> x15, starting transfers between devices: none -> 28.7 us  [extend_the_tasks(): lax.ppermute(y1, axis_name=dev_axis, perm=[(w, (w + m) % row_out) for w i...]
    all_to_all x1 -> x0, waiting for transfers between devices: 11.6 us -> none  [local(): lax.all_to_all(score_slots(arrived), 'idx', split_axis=0, concat_axis=0,...]
    all_to_all x1 -> x0, starting transfers between devices: 10.2 us -> none  [local(): lax.all_to_all(score_slots(arrived), 'idx', split_axis=0, concat_axis=0,...]
  transfers between devices with their start and end apart: 5 -> 19, of which waited for: 4 -> 4; matrix products, arithmetic and copies ran while one was open for 38% -> 37% of each run, Pallas kernels for 0% -> 0%
where the time goes in v1:
time: 407 us; the launch traced here: 399 us
  waiting for transfers between devices  157 us (39%)
  local copies, waits for them, and re-layouts  98.8 us (24%)
  other arithmetic  52.1 us (13%)
  starting transfers between devices  40.8 us (10%)
  matrix products  35.4 us (9%)
  between operations  14.9 us (4%)
    all_gather x1, waiting for transfers between devices, local(): lax.all_gather(qkv_values, 'idx', axis=1, tiled=True)  85.8 us
    all_to_all x1, waiting for transfers between devices, local(): lax.all_to_all(send_rows, 'idx', split_axis=0, concat_axis=0, tiled=True)  34.7 us
    all_gather x1, waiting for transfers between devices, local(): lax.all_gather(proj_values, 'idx', axis=1, tiled=True)  33.5 us
    ppermute x15, starting transfers between devices, extend_the_tasks(): lax.ppermute(y1, axis_name=dev_axis, perm=[(w, (w + m) % row_out) for w i...  28.7 us
    gather x3, local copies, waits for them, and re-layouts, score_slots(): chosen = jnp.take_along_axis(all_scores, block_index[:, :, None], axis=1)  23.3 us
    sub x1, other arithmetic, attend(): logits = logits - jnp.max(logits, axis=-1, keepdims=True)  16.6 us
    dot_general x2, matrix products, project_with(): jnp.dot(left_rows, dequant(col_piece, exponents), preferred_element_type=...  16.4 us
    all_gather x1, local copies, waits for them, and re-layouts, local(): lax.all_gather(qkv_values, 'idx', axis=1, tiled=True)  16 us
  transfers between devices with their start and end apart: 19, of which 4 were waited for; matrix products, arithmetic and copies ran while one was open for 37% of the time, Pallas kernels for 0%

profile of v1, /device:TPU:0, one launch (start us, length us, event | category | flops | bytes accessed | tf_op | source)
XLA Modules:
  0.0 398.9 jit_solution(11818093786819774328)
XLA Ops:
  12.8 4.2 %scatter_custom_fusion = bf16[544,4]{1,0:T(8,128)(2,1)S(1)} fusion(s32[514]{0:T(1024)S(1)} %fusion.30, bf16[514,4]{1,0:T(8,128)(2,1)S(1)} %copy.41, bf16[]{:T(256)} %constant.132.clone.1), kind=kCustom, calls=%fused_computation.41 | custom fusion | bytes 4354 | tf_op jit(solution)/shard_map/scatter | solution.py:137
  17.9 7.4 %all-to-all-start = ((bf16[16,34,4]{1,2,0:T(4,128)(2,1)}), bf16[16,34,4]{1,2,0:T(4,128)(2,1)S(1)}, u32[]{:S(2)}, u32[]{:S(2)}) async-start(bf16[16,34,4]{1,2,0:T(4,128)(2,1)} %copy.43), calls=%async_computation | async-start | bytes 32768 | tf_op jit(solution)/shard_map/all_to_all | solution.py:143
  29.1 33.5 %all-gather.5.cloned.1.call-done = bf16[1408,1408]{0,1:T(8,128)(2,1)} async-done(((bf16[1408,88]{0,1:T(8,128)(2,1)}), bf16[1408,1408]{0,1:T(8,128)(2,1)}) %all-gather.5.cloned.1.call-update) | async-done | bytes 3964944 | tf_op jit(solution)/shard_map/all_gather | solution.py:115
  62.6 6.2 %copy.38 = bf16[1408,1408]{1,0:T(8,128)(2,1)} copy(bf16[1408,1408]{0,1:T(8,128)(2,1)} %all-gather.5.cloned.1.call-done) | data formatting | bytes 7929856 | tf_op jit(solution)/shard_map/all_gather | solution.py:115
  68.8 5.0 %fusion.5 = bf16[1408,1408]{1,0:T(8,128)(2,1)} fusion(bf16[1408,1408]{1,0:T(8,128)(2,1)} %copy.38, f32[11,1408]{1,0:T(8,128)S(1)} %multiply_exponential_fusion.1), kind=kLoop, calls=%fused_computation.13 | loop fusion | flops 5947392 | bytes 7991808 | tf_op jit(solution)/shard_map/convert_element_type | solution.py:48
  73.8 85.8 %all-gather.3.cloned.1.call-done = bf16[1408,4224]{0,1:T(8,128)(2,1)} async-done(((bf16[1408,264]{0,1:T(8,128)(2,1)}), bf16[1408,4224]{0,1:T(8,128)(2,1)}) %all-gather.3.cloned.1.call-update) | async-done | bytes 11894800 | tf_op jit(solution)/shard_map/all_gather | solution.py:111
  159.6 16.0 %copy.32 = bf16[1408,4224]{1,0:T(8,128)(2,1)} copy(bf16[1408,4224]{0,1:T(8,128)(2,1)} %all-gather.3.cloned.1.call-done) | data formatting | bytes 23789568 | tf_op jit(solution)/shard_map/all_gather | solution.py:111
  175.6 6.8 %fusion.1 = bf16[1408,4224]{1,0:T(8,128)(2,1)S(1)} fusion(bf16[1408,4224]{1,0:T(8,128)(2,1)} %copy.32, f32[11,4224]{1,0:T(8,128)S(1)} %multiply_exponential_fusion), kind=kLoop, calls=%fused_computation.7 | loop fusion | flops 17842176 | bytes 23975424 | tf_op jit(solution)/shard_map/convert_element_type | solution.py:48
  182.4 9.2 %convolution_convert_fusion = bf16[514,4224]{1,0:T(8,128)(2,1)} fusion(bf16[1408,4224]{1,0:T(8,128)(2,1)S(1)} %fusion.1, bf16[514,1408]{1,0:T(8,128)(2,1)S(1)} %copy-done.1, f32[1408]{0:T(1024)S(1)} %copy-done.5, f32[514]{0:T(1024)S(1)} %add_rsqrt_fusion.1, f32[514]{0:T(1024)S(1)} %broadcast_multiply_fusion), kind=kOutput, calls=%fused_computation.14 | convolution fusion | flops 6119708672 | bytes 17694224 | tf_op jit(solution)/shard_map/dot_general | solution.py:75
  191.6 14.9 %reshape.165 = bf16[2,257,3,16,88]{4,3,2,1,0:T(8,128)(2,1)} reshape(bf16[514,4224]{1,0:T(8,128)(2,1)} %convolution_convert_fusion) | data formatting | bytes 8684544 | tf_op jit(solution)/shard_map/reshape | solution.py:60
  206.4 5.3 %fusion.34 = (bf16[2,257,1,16,88]{4,3,2,1,0:T(8,128)(2,1)}, bf16[2,257,1,16,88]{4,3,2,1,0:T(8,128)(2,1)S(1)}, bf16[2,257,1,16,88]{4,3,2,1,0:T(8,128)(2,1)S(1)}) fusion(bf16[2,257,3,16,88]{4,3,2,1,0:T(8,128)(2,1)} %reshape.165), kind=kLoop, calls=%fused_computation.104 | loop fusion | bytes 8684544 | tf_op jit(solution)/shard_map/slice | solution.py:69
  211.8 7.2 %fusion.13 = f32[2,16,257,257]{2,3,1,0:T(8,128)} fusion(bf16[2,257,1,16,88]{4,3,2,1,0:T(8,128)(2,1)S(1)} %get-tuple-element.3, bf16[2,257,1,16,88]{4,3,2,1,0:T(8,128)(2,1)S(1)} %get-tuple-element.4), kind=kOutput, calls=%fused_computation.28 | convolution fusion | flops 371987968 | bytes 11349120 | tf_op jit(solution)/shard_map/gqhd,gkhd->ghqk/dot_general | solution.py:61
  218.9 16.6 %fusion.35 = (f32[2,16,257]{2,1,0:T(8,128)S(1)}, f32[2,16,257,257]{2,3,1,0:T(8,128)}) fusion(f32[2,16,257,257]{2,3,1,0:T(8,128)} %fusion.13), kind=kOutput, calls=%fused_computation.105 | output fusion | flops 8454528 | bytes 16941440 | tf_op jit(solution)/shard_map/sub | solution.py:65
  235.6 4.4 %copy.49 = bf16[2,257,1,16,88]{1,4,3,0,2:T(8,128)(2,1)} copy(bf16[2,257,1,16,88]{4,3,2,1,0:T(8,128)(2,1)} %get-tuple-element.2) | data formatting | bytes 2894848
  240.0 8.5 %convert_bitcast_fusion = bf16[2,257,16,88]{1,3,2,0:T(8,128)(2,1)} fusion(f32[2,16,257,257]{2,3,1,0:T(8,128)} %get-tuple-element.22, f32[2,16,257]{2,1,0:T(8,128)S(1)} %get-tuple-element.21, bf16[2,257,1,16,88]{1,4,3,0,2:T(8,128)(2,1)} %copy.49), kind=kOutput, calls=%fused_computation.31 | convolution fusion | flops 376938816 | bytes 11382016 | tf_op jit(solution)/shard_map/ghqk,gkhd->gqhd/dot_general | solution.py:68
  248.5 4.5 %copy.37 = bf16[2,257,16,88]{3,2,1,0:T(8,128)(2,1)} copy(bf16[2,257,16,88]{1,3,2,0:T(8,128)(2,1)} %convert_bitcast_fusion) | data formatting | bytes 2894848 | tf_op jit(solution)/shard_map/convert_element_type | solution.py:71
  253.1 5.1 %reshape.166 = bf16[514,1408]{1,0:T(8,128)(2,1)} reshape(bf16[2,257,16,88]{3,2,1,0:T(8,128)(2,1)} %copy.37) | data formatting | bytes 2894848 | tf_op jit(solution)/shard_map/reshape | solution.py:71
  258.1 7.3 %multiply_reduce_fusion.1 = (f32[514]{0:T(1024)S(1)}, f32[514,1408]{1,0:T(8,128)}) fusion(bf16[514,1408]{1,0:T(8,128)(2,1)} %reshape.166, bf16[1408,1408]{1,0:T(8,128)(2,1)} %fusion.5, bf16[514,1408]{1,0:T(8,128)(2,1)} %param.9), kind=kOutput, calls=%fused_computation.26 | convolution fusion | flops 2040867328 | bytes 9756680 | tf_op jit(solution)/shard_map/dot_general | solution.py:75
  265.4 12.3 %scatter_custom_fusion.1 = bf16[544,1408]{1,0:T(8,128)(2,1)} fusion(s32[514]{0:T(1024)S(1)} %fusion.30, bf16[]{:T(256)} %constant.138.clone.1, f32[514,1408]{1,0:T(8,128)} %get-tuple-element.24, f32[514]{0:T(1024)S(1)} %add_rsqrt_fusion), kind=kCustom, calls=%fused_computation.36 | custom fusion | flops 1447424 | bytes 4430850 | tf_op jit(solution)/shard_map/scatter | solution.py:130
  277.7 2.6 reshape.170
  280.3 4.6 %all-to-all-start.1 = ((bf16[16,34,1408]{2,1,0:T(8,128)(2,1)}), bf16[16,34,1408]{2,1,0:T(8,128)(2,1)}, u32[]{:S(2)}, u32[]{:S(2)}) async-start(bf16[16,34,1408]{2,1,0:T(8,128)(2,1)} %reshape.170), calls=%async_computation.1 | async-start | bytes 3604480 | tf_op jit(solution)/shard_map/all_to_all | solution.py:142
  286.0 34.7 %all-to-all-done.1 = bf16[16,34,1408]{2,1,0:T(8,128)(2,1)} async-done(((bf16[16,34,1408]{2,1,0:T(8,128)(2,1)}), bf16[16,34,1408]{2,1,0:T(8,128)(2,1)}, u32[]{:S(2)}, u32[]{:S(2)}) %all-to-all-start.1) | async-done | bytes 1531936 | tf_op jit(solution)/shard_map/all_to_all | solution.py:142
  320.8 2.6 reshape.215
  323.3 3.3 fusion.36
  328.1 22.9 %gather_fusion.2 = bf16[2176,128]{1,0:T(8,128)(2,1)S(1)} fusion(bf16[544,8,128]{2,1,0:T(8,128)(2,1)} %copy.47, s32[2176]{0:T(1024)S(1)} %reshape.191), kind=kCustom, calls=%fused_computation.2 | custom fusion | bytes 1131520 | tf_op jit(solution)/shard_map/jit(take_along_axis)/gather | solution.py:91
  353.1 3.2 multiply_convert_fusion
  356.3 2.9 collective-permute-start.1
  359.2 5.4 %collective-permute-start.2 = (bf16[1,34,4,128]{3,2,1,0:T(4,128)(2,1)S(1)}, bf16[1,34,4,128]{3,2,1,0:T(4,128)(2,1)S(1)}, u32[]{:S(2)}, u32[]{:S(2)}) collective-permute-start(bf16[1,34,4,128]{3,2,1,0:T(4,128)(2,1)S(1)} %get-tuple-element.17), channel_id=1, source_target_pairs={{0,3},{1,4},{2,5},{3,6},{4,7},{5,8},{6,9},{7,10},{8,11},{9,12},{10... | collective-permute-start | bytes 104456 | tf_op jit(solution)/shard_map/ppermute | solution.py:34
  367.0 3.7 collective-permute-start.6
  374.8 2.7 collective-permute-start.10
  380.8 3.5 collective-permute-start.14
  388.8 3.1 gather_fusion.1
  (93 shorter events, 28.7 us)
Async XLA Ops:
  7.2 316.2 %copy-start = (bf16[1024,1408]{1,0:T(8,128)(2,1)S(1)}, bf16[1024,1408]{1,0:T(8,128)(2,1)}, u32[]{:S(2)}) copy-start(bf16[1024,1408]{1,0:T(8,128)(2,1)} %param.15) | copy-start | bytes 8650756
  7.2 21.8 %copy-start.3 = (s32[11,4224]{1,0:T(8,128)S(1)}, s32[11,4224]{1,0:T(8,128)}, u32[]{:S(2)}) copy-start(s32[11,4224]{1,0:T(8,128)} %param.12) | copy-start | bytes 557572
  7.2 55.4 %all-gather.5.cloned.1.call-start = ((), (), s32[]{:S(2)}) async-start(), calls=%async_computation.3 | async-start | bytes 4212736 | tf_op jit(solution)/shard_map/all_gather | solution.py:115
  7.9 151.7 %all-gather.3.cloned.1.call-start = ((), (), s32[]{:S(2)}) async-start(), calls=%async_computation.2 | async-start | bytes 12638208 | tf_op jit(solution)/shard_map/all_gather | solution.py:111
  17.1 11.9 %copy-start.4 = (s32[11,1408]{1,0:T(8,128)S(1)}, s32[11,1408]{1,0:T(8,128)}, u32[]{:S(2)}) copy-start(s32[11,1408]{1,0:T(8,128)} %param.14) | copy-start | bytes 185860
  17.9 262.4 %all-to-all-start = ((bf16[16,34,4]{1,2,0:T(4,128)(2,1)}), bf16[16,34,4]{1,2,0:T(4,128)(2,1)S(1)}, u32[]{:S(2)}, u32[]{:S(2)}) async-start(bf16[16,34,4]{1,2,0:T(4,128)(2,1)} %copy.43), calls=%async_computation | async-start | bytes 32768 | tf_op jit(solution)/shard_map/all_to_all | solution.py:143
  175.5 6.8 %copy-start.1 = (bf16[514,1408]{1,0:T(8,128)(2,1)S(1)}, bf16[514,1408]{1,0:T(8,128)(2,1)}, u32[]{:S(2)}) copy-start(bf16[514,1408]{1,0:T(8,128)(2,1)} %param.9) | copy-start | bytes 4342276
  175.6 6.8 %copy-start.5 = (f32[1408]{0:T(1024)S(1)}, f32[1408]{0:T(1024)}, u32[]{:S(2)}) copy-start(f32[1408]{0:T(1024)} %param.10) | copy-start | bytes 16900
  280.3 40.4 %all-to-all-start.1 = ((bf16[16,34,1408]{2,1,0:T(8,128)(2,1)}), bf16[16,34,1408]{2,1,0:T(8,128)(2,1)}, u32[]{:S(2)}, u32[]{:S(2)}) async-start(bf16[16,34,1408]{2,1,0:T(8,128)(2,1)} %reshape.170), calls=%async_computation.1 | async-start | bytes 3604480 | tf_op jit(solution)/shard_map/all_to_all | solution.py:142
  352.1 13.3 %collective-permute-start = (bf16[1,34,4,128]{3,2,1,0:T(4,128)(2,1)S(1)}, bf16[1,34,4,128]{3,2,1,0:T(4,128)(2,1)S(1)}, u32[]{:S(2)}, u32[]{:S(2)}) collective-permute-start(bf16[1,34,4,128]{3,2,1,0:T(4,128)(2,1)S(1)} %get-tuple-element.19), channel_id=1, source_target_pairs={{0,1},{1,2},{2,3},{3,4},{4,5},{5,6},{6,7},{7,8},{8,9},{9,10},{10,1... | collective-permute-start | bytes 104456 | tf_op jit(solution)/shard_map/ppermute | solution.py:34
  356.3 10.7 %collective-permute-start.1 = (bf16[1,34,4,128]{3,2,1,0:T(4,128)(2,1)S(1)}, bf16[1,34,4,128]{3,2,1,0:T(4,128)(2,1)S(1)}, u32[]{:S(2)}, u32[]{:S(2)}) collective-permute-start(bf16[1,34,4,128]{3,2,1,0:T(4,128)(2,1)S(1)} %get-tuple-element.18), channel_id=1, source_target_pairs={{0,2},{1,3},{2,4},{3,5},{4,6},{5,7},{6,8},{7,9},{8,10},{9,11},{10,... | collective-permute-start | bytes 104456 | tf_op jit(solution)/shard_map/ppermute | solution.py:34
  359.2 11.5 %collective-permute-start.2 = (bf16[1,34,4,128]{3,2,1,0:T(4,128)(2,1)S(1)}, bf16[1,34,4,128]{3,2,1,0:T(4,128)(2,1)S(1)}, u32[]{:S(2)}, u32[]{:S(2)}) collective-permute-start(bf16[1,34,4,128]{3,2,1,0:T(4,128)(2,1)S(1)} %get-tuple-element.17), channel_id=1, source_target_pairs={{0,3},{1,4},{2,5},{3,6},{4,7},{5,8},{6,9},{7,10},{8,11},{9,12},{10... | collective-permute-start | bytes 104456 | tf_op jit(solution)/shard_map/ppermute | solution.py:34
  364.6 6.5 %collective-permute-start.3 = (bf16[1,34,4,128]{3,2,1,0:T(4,128)(2,1)S(1)}, bf16[1,34,4,128]{3,2,1,0:T(4,128)(2,1)S(1)}, u32[]{:S(2)}, u32[]{:S(2)}) collective-permute-start(bf16[1,34,4,128]{3,2,1,0:T(4,128)(2,1)S(1)} %get-tuple-element.16), channel_id=1, source_target_pairs={{0,4},{1,5},{2,6},{3,7},{4,8},{5,9},{6,10},{7,11},{8,12},{9,13},{1... | collective-permute-start | bytes 104456 | tf_op jit(solution)/shard_map/ppermute | solution.py:34
  365.2 7.7 %collective-permute-start.4 = (bf16[1,34,4,128]{3,2,1,0:T(4,128)(2,1)S(1)}, bf16[1,34,4,128]{3,2,1,0:T(4,128)(2,1)S(1)}, u32[]{:S(2)}, u32[]{:S(2)}) collective-permute-start(bf16[1,34,4,128]{3,2,1,0:T(4,128)(2,1)S(1)} %get-tuple-element.15), channel_id=1, source_target_pairs={{0,5},{1,6},{2,7},{3,8},{4,9},{5,10},{6,11},{7,12},{8,13},{9,14},{... | collective-permute-start | bytes 104456 | tf_op jit(solution)/shard_map/ppermute | solution.py:34
  365.4 9.4 %collective-permute-start.5 = (bf16[1,34,4,128]{3,2,1,0:T(4,128)(2,1)S(1)}, bf16[1,34,4,128]{3,2,1,0:T(4,128)(2,1)S(1)}, u32[]{:S(2)}, u32[]{:S(2)}) collective-permute-start(bf16[1,34,4,128]{3,2,1,0:T(4,128)(2,1)S(1)} %get-tuple-element.14), channel_id=1, source_target_pairs={{0,6},{1,7},{2,8},{3,9},{4,10},{5,11},{6,12},{7,13},{8,14},{9,15},... | collective-permute-start | bytes 104456 | tf_op jit(solution)/shard_map/ppermute | solution.py:34
  367.0 10.5 %collective-permute-start.6 = (bf16[1,34,4,128]{3,2,1,0:T(4,128)(2,1)S(1)}, bf16[1,34,4,128]{3,2,1,0:T(4,128)(2,1)S(1)}, u32[]{:S(2)}, u32[]{:S(2)}) collective-permute-start(bf16[1,34,4,128]{3,2,1,0:T(4,128)(2,1)S(1)} %get-tuple-element.13), channel_id=1, source_target_pairs={{0,7},{1,8},{2,9},{3,10},{4,11},{5,12},{6,13},{7,14},{8,15},{9,0},... | collective-permute-start | bytes 104456 | tf_op jit(solution)/shard_map/ppermute | solution.py:34
  370.7 8.4 %collective-permute-start.7 = (bf16[1,34,4,128]{3,2,1,0:T(4,128)(2,1)S(1)}, bf16[1,34,4,128]{3,2,1,0:T(4,128)(2,1)S(1)}, u32[]{:S(2)}, u32[]{:S(2)}) collective-permute-start(bf16[1,34,4,128]{3,2,1,0:T(4,128)(2,1)S(1)} %get-tuple-element.12), channel_id=1, source_target_pairs={{0,8},{1,9},{2,10},{3,11},{4,12},{5,13},{6,14},{7,15},{8,0},{9,1},... | collective-permute-start | bytes 104456 | tf_op jit(solution)/shard_map/ppermute | solution.py:34
  371.1 8.4 %collective-permute-start.8 = (bf16[1,34,4,128]{3,2,1,0:T(4,128)(2,1)S(1)}, bf16[1,34,4,128]{3,2,1,0:T(4,128)(2,1)S(1)}, u32[]{:S(2)}, u32[]{:S(2)}) collective-permute-start(bf16[1,34,4,128]{3,2,1,0:T(4,128)(2,1)S(1)} %get-tuple-element.11), channel_id=1, source_target_pairs={{0,9},{1,10},{2,11},{3,12},{4,13},{5,14},{6,15},{7,0},{8,1},{9,2},... | collective-permute-start | bytes 104456 | tf_op jit(solution)/shard_map/ppermute | solution.py:34
  372.9 7.9 %collective-permute-start.9 = (bf16[1,34,4,128]{3,2,1,0:T(4,128)(2,1)S(1)}, bf16[1,34,4,128]{3,2,1,0:T(4,128)(2,1)S(1)}, u32[]{:S(2)}, u32[]{:S(2)}) collective-permute-start(bf16[1,34,4,128]{3,2,1,0:T(4,128)(2,1)S(1)} %get-tuple-element.10), channel_id=1, source_target_pairs={{0,10},{1,11},{2,12},{3,13},{4,14},{5,15},{6,0},{7,1},{8,2},{9,3},... | collective-permute-start | bytes 104456 | tf_op jit(solution)/shard_map/ppermute | solution.py:34
  374.8 9.5 %collective-permute-start.10 = (bf16[1,34,4,128]{3,2,1,0:T(4,128)(2,1)S(1)}, bf16[1,34,4,128]{3,2,1,0:T(4,128)(2,1)S(1)}, u32[]{:S(2)}, u32[]{:S(2)}) collective-permute-start(bf16[1,34,4,128]{3,2,1,0:T(4,128)(2,1)S(1)} %get-tuple-element.9), channel_id=1, source_target_pairs={{0,11},{1,12},{2,13},{3,14},{4,15},{5,0},{6,1},{7,2},{8,3},{9,4},{... | collective-permute-start | bytes 104456 | tf_op jit(solution)/shard_map/ppermute | solution.py:34
  377.5 6.8 %collective-permute-start.11 = (bf16[1,34,4,128]{3,2,1,0:T(4,128)(2,1)S(1)}, bf16[1,34,4,128]{3,2,1,0:T(4,128)(2,1)S(1)}, u32[]{:S(2)}, u32[]{:S(2)}) collective-permute-start(bf16[1,34,4,128]{3,2,1,0:T(4,128)(2,1)S(1)} %get-tuple-element.8), channel_id=1, source_target_pairs={{0,12},{1,13},{2,14},{3,15},{4,0},{5,1},{6,2},{7,3},{8,4},{9,5},{1... | collective-permute-start | bytes 104456 | tf_op jit(solution)/shard_map/ppermute | solution.py:34
  379.1 5.3 %collective-permute-start.12 = (bf16[1,34,4,128]{3,2,1,0:T(4,128)(2,1)S(1)}, bf16[1,34,4,128]{3,2,1,0:T(4,128)(2,1)S(1)}, u32[]{:S(2)}, u32[]{:S(2)}) collective-permute-start(bf16[1,34,4,128]{3,2,1,0:T(4,128)(2,1)S(1)} %get-tuple-element.7), channel_id=1, source_target_pairs={{0,13},{1,14},{2,15},{3,0},{4,1},{5,2},{6,3},{7,4},{8,5},{9,6},{10... | collective-permute-start | bytes 104456 | tf_op jit(solution)/shard_map/ppermute | solution.py:34
  379.5 4.9 %collective-permute-start.13 = (bf16[1,34,4,128]{3,2,1,0:T(4,128)(2,1)S(1)}, bf16[1,34,4,128]{3,2,1,0:T(4,128)(2,1)S(1)}, u32[]{:S(2)}, u32[]{:S(2)}) collective-permute-start(bf16[1,34,4,128]{3,2,1,0:T(4,128)(2,1)S(1)} %get-tuple-element.6), channel_id=1, source_target_pairs={{0,14},{1,15},{2,0},{3,1},{4,2},{5,3},{6,4},{7,5},{8,6},{9,7},{10,... | collective-permute-start | bytes 104456 | tf_op jit(solution)/shard_map/ppermute | solution.py:34
  380.8 5.1 %collective-permute-start.14 = (bf16[1,34,4,128]{3,2,1,0:T(4,128)(2,1)S(1)}, bf16[1,34,4,128]{3,2,1,0:T(4,128)(2,1)S(1)}, u32[]{:S(2)}, u32[]{:S(2)}) collective-permute-start(bf16[1,34,4,128]{3,2,1,0:T(4,128)(2,1)S(1)} %get-tuple-element.5), channel_id=1, source_target_pairs={{0,15},{1,0},{2,1},{3,2},{4,3},{5,4},{6,5},{7,6},{8,7},{9,8},{10,9... | collective-permute-start | bytes 104456 | tf_op jit(solution)/shard_map/ppermute | solution.py:34
  385.9 0.8 copy-start.2
Sparse Core Ops, SparseCore 0:
  10.2 52.3 all-gather.4
  64.7 94.8 all-gather.2
